TPU v7x, 512 devices: a whole 4x4x16 slice. The times are simulated.
512 devices in a mesh: row: 8 (over z_hi, core), col: 16 (over y, z_lo), depth: 4 (over x).
Axes of the slice: x: 4, y: 4, z: 16 (z_hi: 4, z_lo: 4; z = z_hi * 4 + z_lo), core: 2. Of those that a mesh axis runs over, the one named last changes fastest.
Arguments:
- values: bfloat16 [768, 16, 128, 128], P(('row', 'col')), may hold values from -0.47851562 to 0.47851562
- columns: int32 [768, 16], replicated, may hold values from 0 to 767, as said below
Outputs:
- purified: bfloat16 [768, 16, 128, 128], P(('row', 'col'), 'depth')
Inputs may be any that keep to these rules, and one draw needn't show every extreme that they name: Each block row a names 16 different block columns, a itself among them, all within 8 of a around the cycle of 768 block rows (indices wrap).
All inputs are finite; a program needn't handle non-finite values.
Results may differ from a plain program's by a relative error of at most 0.0047.
Values may be sent and summed in bfloat16 or wider, within the bound.
A program may use at most 128 MiB of HBM per device.

v0:
```python
import jax
import jax.numpy as jnp
from jax import lax
from jax.sharding import PartitionSpec as P

HB = 8


def passed_along(value, axis, by):
    peers = lax.axis_size(axis)
    return lax.ppermute(value, axis, [(i, (i + by) % peers) for i in range(peers)])


def matched_blocks(nearby, band_start, own_cols, target_cols, columns):
    total_blocks = columns.shape[0]
    band_count = nearby.shape[0]
    slot_count = nearby.shape[1]
    partner_cols = jnp.take(columns, own_cols, axis=0)
    same_column = partner_cols[:, :, None, :] == target_cols[:, None, :, None]
    slot_ids = jnp.arange(slot_count, dtype=jnp.int32)
    present = jnp.any(same_column, axis=3)
    chosen = jnp.sum(jnp.where(same_column, slot_ids, 0), axis=3)
    offset = jnp.mod(own_cols - band_start, total_blocks)
    inside = offset < band_count
    usable = inside[:, :, None] & present
    flat_index = jnp.where(
        usable, offset[:, :, None] * slot_count + chosen, band_count * slot_count
    )
    flat_blocks = nearby.reshape(band_count * slot_count, nearby.shape[2], nearby.shape[3])
    return jnp.take(flat_blocks, flat_index, axis=0, mode="fill", fill_value=0)


def local(values, columns):
    own_rows, slot_count, block_size, _ = values.shape
    layers = lax.axis_size("depth")
    quarter = slot_count // layers
    layer_index = lax.axis_index("depth")
    group_index = lax.axis_index(("row", "col"))
    first_row = group_index * own_rows
    own_cols = lax.dynamic_slice_in_dim(columns, first_row, own_rows, 0)
    target_cols = lax.dynamic_slice_in_dim(own_cols, layer_index * quarter, quarter, 1)
    hop_count = (HB + own_rows - 1) // own_rows
    reach_last = HB - (hop_count - 1) * own_rows
    lower_parts = []
    upper_parts = []
    for hop_step in range(1, hop_count + 1):
        edge_rows = own_rows if hop_step < hop_count else reach_last
        from_lower = passed_along(values[own_rows - edge_rows :], ("row", "col"), hop_step)
        from_upper = passed_along(values[:edge_rows], ("row", "col"), -hop_step)
        lower_parts.insert(0, from_lower)
        upper_parts.append(from_upper)
    below_rows = jnp.concatenate(lower_parts, axis=0)
    above_rows = jnp.concatenate(upper_parts, axis=0)
    nearby = jnp.concatenate([below_rows, values, above_rows], axis=0)
    selected = matched_blocks(nearby, first_row - HB, own_cols, target_cols, columns)
    square32 = jnp.einsum("aixy,aijyz->ajxz", values, selected, preferred_element_type=jnp.float32)
    square = square32.astype(jnp.bfloat16)
    whole_square = lax.all_gather(square, "depth", axis=1, tiled=True)
    cube32 = jnp.einsum(
        "aixy,aijyz->ajxz", whole_square, selected, preferred_element_type=jnp.float32
    )
    return (3.0 * square32 - 2.0 * cube32).astype(jnp.bfloat16)


def solution(mesh):
    placed = (P(("row", "col"), None, None, None), P())
    return jax.shard_map(
        local,
        mesh=mesh,
        in_specs=placed,
        out_specs=P(("row", "col"), "depth", None, None),
        check_vma=False,
    )
```

profile of v0, /device:TPU:1, one launch (start us, length us, event | category | flops | bytes accessed | tf_op | source)
XLA Modules:
  0.0 335.9 jit_solution(13076159911926167194)
XLA Ops:
  6.5 4.6 %collective-permute-start.1 = (bf16[6,16,128,128]{3,2,1,0:T(8,128)(2,1)}, bf16[6,16,128,128]{3,2,1,0:T(8,128)(2,1)}, u32[]{:S(2)}, u32[]{:S(2)}) collective-permute-start(bf16[6,16,128,128]{3,2,1,0:T(8,128)(2,1)} %param.2), channel_id=1, source_target_pairs={{0,4},{4,8},{8,12},{12,16},{16,20},{20,24},{24,28},{28,32},{32,36}... | collective-permute-start | bytes 9437192 | tf_op jit(solution)/shard_map/ppermute | solution.py:11
  11.2 7.6 %collective-permute-start.2 = (bf16[6,16,128,128]{3,2,1,0:T(8,128)(2,1)}, bf16[6,16,128,128]{3,2,1,0:T(8,128)(2,1)}, u32[]{:S(2)}, u32[]{:S(2)}) collective-permute-start(bf16[6,16,128,128]{3,2,1,0:T(8,128)(2,1)} %param.2), channel_id=1, source_target_pairs={{0,508},{4,0},{8,4},{12,8},{16,12},{20,16},{24,20},{28,24},{32,28}... | collective-permute-start | bytes 9437192 | tf_op jit(solution)/shard_map/ppermute | solution.py:11
  18.8 3.2 fusion.18
  22.0 1.9 collective-permute-start
  23.9 6.7 %collective-permute-start.3 = (bf16[2,16,128,128]{3,2,1,0:T(8,128)(2,1)}, bf16[2,16,128,128]{3,2,1,0:T(8,128)(2,1)}, u32[]{:S(2)}, u32[]{:S(2)}) collective-permute-start(bf16[2,16,128,128]{3,2,1,0:T(8,128)(2,1)} %get-tuple-element.7), channel_id=1, source_target_pairs={{0,504},{4,508},{8,0},{12,4},{16,8},{20,12},{24,16},{28,20},{32,24... | collective-permute-start | bytes 3145736 | tf_op jit(solution)/shard_map/ppermute | solution.py:11
  30.6 1.0 copy.39
  33.3 1.4 dynamic_slice.7
  34.7 0.8 copy.41
  35.5 1.2 gather_fusion
  36.7 0.9 broadcast_select_fusion.7
  39.1 138.4 %collective-permute-done = bf16[2,16,128,128]{3,2,1,0:T(8,128)(2,1)} collective-permute-done((bf16[2,16,128,128]{3,2,1,0:T(8,128)(2,1)}, bf16[2,16,128,128]{3,2,1,0:T(8,128)(2,1)}, u32[]{:S(2)}, u32[]{:S(2)}) %collective-permute-start) | collective-permute-done | bytes 1048608 | tf_op jit(solution)/shard_map/ppermute | solution.py:11
  177.5 2.4 constant_dynamic-update-slice_fusion.4
  179.8 3.9 %constant_dynamic-update-slice_fusion.3 = bf16[22,16,128,128]{3,2,1,0:T(8,128)(2,1)} fusion(bf16[22,16,128,128]{3,2,1,0:T(8,128)(2,1)} %constant_dynamic-update-slice_fusion.4, bf16[6,16,128,128]{3,2,1,0:T(8,128)(2,1)} %collective-permute-done.1), kind=kLoop, calls=%fused_computation.30 | loop fusion | bytes 6291456
  183.8 2.1 constant_dynamic-update-slice_fusion.2
  185.9 4.0 %constant_dynamic-update-slice_fusion.1 = bf16[22,16,128,128]{3,2,1,0:T(8,128)(2,1)} fusion(bf16[22,16,128,128]{3,2,1,0:T(8,128)(2,1)} %constant_dynamic-update-slice_fusion.2, bf16[6,16,128,128]{3,2,1,0:T(8,128)(2,1)} %collective-permute-done.2), kind=kLoop, calls=%fused_computation.28 | loop fusion | bytes 6291456
  189.8 50.2 %collective-permute-done.3 = bf16[2,16,128,128]{3,2,1,0:T(8,128)(2,1)} collective-permute-done((bf16[2,16,128,128]{3,2,1,0:T(8,128)(2,1)}, bf16[2,16,128,128]{3,2,1,0:T(8,128)(2,1)}, u32[]{:S(2)}, u32[]{:S(2)}) %collective-permute-start.3) | collective-permute-done | bytes 1048608 | tf_op jit(solution)/shard_map/ppermute | solution.py:11
  240.1 2.3 constant_dynamic-update-slice_fusion
  242.4 15.5 %gather_fusion.1 = bf16[384,128,128]{2,1,0:T(8,128)(2,1)} fusion(bf16[352,128,128]{2,1,0:T(8,128)(2,1)} %bitcast.1, s32[1024]{0:T(1024)S(1)} %pad_clamp_fusion), kind=kCustom, calls=%fused_computation.1 | custom fusion | bytes 25167360 | tf_op jit(solution)/shard_map/jit(_take)/gather | solution.py:30
  257.9 7.9 %fusion = f32[6,4,128,128,1]{3,2,1,4,0:T(8,128)S(1)} fusion(bf16[6,16,4,128,128]{4,3,2,1,0:T(8,128)(2,1)} %bitcast.62, pred[6,16,4]{2,1,0:T(8,128)(4,1)S(1)} %copy.42, bf16[6,16,128,128]{3,2,1,0:T(8,128)(2,1)S(1)} %copy-done), kind=kOutput, calls=%fused_computation.3 | convolution fusion | flops 1616904192 | bytes 17301888 | tf_op jit(solution)/shard_map/aixy,aijyz->ajxz/dot_general | solution.py:56
  265.8 1.1 copy-done.1
  266.9 1.0 fusion.13
  268.0 51.1 %all-gather.2.cloned.1.call-done = bf16[6,16,128,128]{2,3,1,0:T(8,128)(2,1)} async-done(((bf16[6,4,128,128]{2,3,1,0:T(8,128)(2,1)}), bf16[6,16,128,128]{2,3,1,0:T(8,128)(2,1)}) %all-gather.2.cloned.1.call-update) | async-done | bytes 3145744 | tf_op jit(solution)/shard_map/all_gather | solution.py:58
  319.1 8.7 %fusion.10 = bf16[6,4,128,128]{2,3,1,0:T(8,128)(2,1)S(1)} fusion(bf16[6,16,128,128]{2,3,1,0:T(8,128)(2,1)} %all-gather.2.cloned.1.call-done, bf16[6,16,4,128,128]{4,3,2,1,0:T(8,128)(2,1)} %bitcast.63, pred[6,16,4]{2,1,0:T(8,128)(4,1)S(1)} %copy.42, f32[6,4,128,128,1]{3,2,1,4,0:T(8,128)} %copy-done.1), kind=kOutput, calls=%fused_computation.14 | convolution fusion | flops 1618477056 | bytes 18088320 | tf_op jit(solution)/shard_map/aixy,aijyz->ajxz/dot_general | solution.py:59
  327.9 1.2 copy.47
  (19 shorter events, 3.4 us)
Async XLA Ops:
  6.5 177.3 %copy-start = (bf16[6,16,128,128]{3,2,1,0:T(8,128)(2,1)S(1)}, bf16[6,16,128,128]{3,2,1,0:T(8,128)(2,1)}, u32[]{:S(2)}) copy-start(bf16[6,16,128,128]{3,2,1,0:T(8,128)(2,1)} %param.2) | copy-start | bytes 9437188
  6.5 312.6 %all-gather.2.cloned.1.call-start = ((), (), s32[]{:S(2)}) async-start(), calls=%async_computation | async-start | bytes 3932160 | tf_op jit(solution)/shard_map/all_gather | solution.py:58
  6.5 173.3 %collective-permute-start.1 = (bf16[6,16,128,128]{3,2,1,0:T(8,128)(2,1)}, bf16[6,16,128,128]{3,2,1,0:T(8,128)(2,1)}, u32[]{:S(2)}, u32[]{:S(2)}) collective-permute-start(bf16[6,16,128,128]{3,2,1,0:T(8,128)(2,1)} %param.2), channel_id=1, source_target_pairs={{0,4},{4,8},{8,12},{12,16},{16,20},{20,24},{24,28},{28,32},{32,36}... | collective-permute-start | bytes 9437192 | tf_op jit(solution)/shard_map/ppermute | solution.py:11
  11.2 174.7 %collective-permute-start.2 = (bf16[6,16,128,128]{3,2,1,0:T(8,128)(2,1)}, bf16[6,16,128,128]{3,2,1,0:T(8,128)(2,1)}, u32[]{:S(2)}, u32[]{:S(2)}) collective-permute-start(bf16[6,16,128,128]{3,2,1,0:T(8,128)(2,1)} %param.2), channel_id=1, source_target_pairs={{0,508},{4,0},{8,4},{12,8},{16,12},{20,16},{24,20},{28,24},{32,28}... | collective-permute-start | bytes 9437192 | tf_op jit(solution)/shard_map/ppermute | solution.py:11
  22.0 155.5 %collective-permute-start = (bf16[2,16,128,128]{3,2,1,0:T(8,128)(2,1)}, bf16[2,16,128,128]{3,2,1,0:T(8,128)(2,1)}, u32[]{:S(2)}, u32[]{:S(2)}) collective-permute-start(bf16[2,16,128,128]{3,2,1,0:T(8,128)(2,1)} %get-tuple-element.8), channel_id=1, source_target_pairs={{0,8},{4,12},{8,16},{12,20},{16,24},{20,28},{24,32},{28,36},{32,40... | collective-permute-start | bytes 3145736 | tf_op jit(solution)/shard_map/ppermute | solution.py:11
  23.9 216.2 %collective-permute-start.3 = (bf16[2,16,128,128]{3,2,1,0:T(8,128)(2,1)}, bf16[2,16,128,128]{3,2,1,0:T(8,128)(2,1)}, u32[]{:S(2)}, u32[]{:S(2)}) collective-permute-start(bf16[2,16,128,128]{3,2,1,0:T(8,128)(2,1)} %get-tuple-element.7), channel_id=1, source_target_pairs={{0,504},{4,508},{8,0},{12,4},{16,8},{20,12},{24,16},{28,20},{32,24... | collective-permute-start | bytes 3145736 | tf_op jit(solution)/shard_map/ppermute | solution.py:11
  265.8 1.1 copy-start.1
Sparse Core Ops, SparseCore 0:
  268.1 50.9 all-gather.1
where the time goes:
time: 336 us
  waiting for transfers between devices  240 us (71%)
  local copies, waits for them, and re-layouts  40.9 us (12%)
  starting transfers between devices  20.8 us (6%)
  matrix products  16.6 us (5%)
  between operations  13.5 us (4%)
  other arithmetic  4.28 us (1%)
    ppermute x4, waiting for transfers between devices, passed_along(): lax.ppermute(value, axis, [(i, (i + by) % peers) for i in range(peers)])  189 us
    all_gather x1, waiting for transfers between devices, local(): whole_square = lax.all_gather(square, 'depth', axis=1, tiled=True)  51.1 us
    ppermute x4, starting transfers between devices, passed_along(): lax.ppermute(value, axis, [(i, (i + by) % peers) for i in range(peers)])  20.8 us
    gather x1, local copies, waits for them, and re-layouts, matched_blocks(): return jnp.take(flat_blocks, flat_index, axis=0, mode='fill', fill_value=0)  15.5 us
    unnamed x9, local copies, waits for them, and re-layouts  14.4 us
    dot_general x1, matrix products, local(): jnp.einsum('aixy,aijyz->ajxz', whole_square, selected, preferred_element_...  8.72 us
    dot_general x1, matrix products, local(): jnp.einsum('aixy,aijyz->ajxz', values, selected, preferred_element_type=j...  7.87 us
  transfers between devices with their start and end apart: 5, of which 3 were waited for; matrix products, arithmetic and copies ran while one was open for 7% of the time, Pallas kernels for 0%

commit v1 on v0

--- a/solution.py
+++ b/solution.py
@@ -55,7 +55,24 @@
     selected = matched_blocks(nearby, first_row - HB, own_cols, target_cols, columns)
     square32 = jnp.einsum("aixy,aijyz->ajxz", values, selected, preferred_element_type=jnp.float32)
     square = square32.astype(jnp.bfloat16)
-    whole_square = lax.all_gather(square, "depth", axis=1, tiled=True)
+    ways, here, step = (lax.axis_size("depth"), lax.axis_index("depth"), square.shape[1])
+    dims = [n * ways if d == 1 else n for d, n in enumerate(square.shape)]
+    whole_square = lax.dynamic_update_slice_in_dim(
+        jnp.zeros(dims, square.dtype), square, here * step, axis=1
+    )
+    going_up = going_down = square
+    for far in range(1, ways // 2 + 1):
+        going_up = lax.ppermute(going_up, "depth", [(d, (d + 1) % ways) for d in range(ways)])
+        whole_square = lax.dynamic_update_slice_in_dim(
+            whole_square, going_up, (here - far) % ways * step, axis=1
+        )
+        if 2 * far < ways:
+            going_down = lax.ppermute(
+                going_down, "depth", [(d, (d - 1) % ways) for d in range(ways)]
+            )
+            whole_square = lax.dynamic_update_slice_in_dim(
+                whole_square, going_down, (here + far) % ways * step, axis=1
+            )
     cube32 = jnp.einsum(
         "aixy,aijyz->ajxz", whole_square, selected, preferred_element_type=jnp.float32
     )

time: 336 us -> 316 us (0.940)
  waiting for transfers between devices: 240 us -> 223 us
  between operations: 13.5 us -> 0.28 us
  starting transfers between devices: 20.8 us -> 29.3 us
  local copies, waits for them, and re-layouts: 40.9 us -> 44.5 us
    all_gather x1 -> x0, waiting for transfers between devices: 51.1 us -> none  [local(): whole_square = lax.all_gather(square, 'depth', axis=1, tiled=True)]
    ppermute x0 -> x3, waiting for transfers between devices: none -> 26.5 us  [the longest x2 26.5 us: local(): lax.ppermute(going_up, 'depth', [(d, (d + 1) % ways) for d in range(ways)])]
    ppermute x0 -> x3, starting transfers between devices: none -> 8.59 us  [the longest x2 5.15 us: local(): lax.ppermute(going_up, 'depth', [(d, (d + 1) % ways) for d in range(ways)])]
    ppermute x4, waiting for transfers between devices: 189 us -> 196 us  [passed_along(): lax.ppermute(value, axis, [(i, (i + by) % peers) for i in range(peers)])]
    dynamic_update_slice x0 -> x4, local copies, waits for them, and re-layouts: none -> 4.14 us  [the longest x2 2.08 us: local(): lax.dynamic_update_slice_in_dim(whole_square, going_up, (here - far) % wa...]
    ppermute x0 -> x3, local copies, waits for them, and re-layouts: none -> 3.39 us  [the longest x2 3.01 us: local(): lax.ppermute(going_up, 'depth', [(d, (d + 1) % ways) for d in range(ways)])]
    unnamed x9 -> x13, local copies, waits for them, and re-layouts: 14.4 us -> 11.2 us
  transfers between devices with their start and end apart: 5 -> 7, of which waited for: 3 -> 4; matrix products, arithmetic and copies ran while one was open for 7% -> 8% of each run, Pallas kernels for 0% -> 0%
where the time goes in v1:
time: 316 us; the launch traced here: 314 us
  waiting for transfers between devices  223 us (71%)
  local copies, waits for them, and re-layouts  44.5 us (14%)
  starting transfers between devices  29.3 us (9%)
  matrix products  16.3 us (5%)
    ppermute x4, waiting for transfers between devices, passed_along(): lax.ppermute(value, axis, [(i, (i + by) % peers) for i in range(peers)])  196 us
    ppermute x2, waiting for transfers between devices, local(): lax.ppermute(going_up, 'depth', [(d, (d + 1) % ways) for d in range(ways)])  26.5 us
    ppermute x4, starting transfers between devices, passed_along(): lax.ppermute(value, axis, [(i, (i + by) % peers) for i in range(peers)])  20.7 us
    gather x1, local copies, waits for them, and re-layouts, matched_blocks(): return jnp.take(flat_blocks, flat_index, axis=0, mode='fill', fill_value=0)  15.5 us
    unnamed x13, local copies, waits for them, and re-layouts  11.2 us
    dot_general x1, matrix products, local(): jnp.einsum('aixy,aijyz->ajxz', whole_square, selected, preferred_element_...  8.47 us
    dot_general x1, matrix products, local(): jnp.einsum('aixy,aijyz->ajxz', values, selected, preferred_element_type=j...  7.87 us
  transfers between devices with their start and end apart: 7, of which 4 were waited for; matrix products, arithmetic and copies ran while one was open for 8% of the time, Pallas kernels for 0%

profile of v1, /device:TPU:1, one launch (start us, length us, event | category | flops | bytes accessed | tf_op | source)
XLA Modules:
  0.0 314.4 jit_solution(13982250647826874787)
XLA Ops:
  0.0 4.5 %collective-permute-start.1 = (bf16[6,16,128,128]{3,2,1,0:T(8,128)(2,1)}, bf16[6,16,128,128]{3,2,1,0:T(8,128)(2,1)}, u32[]{:S(2)}, u32[]{:S(2)}) collective-permute-start(bf16[6,16,128,128]{3,2,1,0:T(8,128)(2,1)} %param.2), channel_id=1, source_target_pairs={{0,4},{4,8},{8,12},{12,16},{16,20},{20,24},{24,28},{28,32},{32,36}... | collective-permute-start | bytes 9437192 | tf_op jit(solution)/shard_map/ppermute | solution.py:11
  4.5 7.6 %collective-permute-start.2 = (bf16[6,16,128,128]{3,2,1,0:T(8,128)(2,1)}, bf16[6,16,128,128]{3,2,1,0:T(8,128)(2,1)}, u32[]{:S(2)}, u32[]{:S(2)}) collective-permute-start(bf16[6,16,128,128]{3,2,1,0:T(8,128)(2,1)} %param.2), channel_id=1, source_target_pairs={{0,508},{4,0},{8,4},{12,8},{16,12},{20,16},{24,20},{28,24},{32,28}... | collective-permute-start | bytes 9437192 | tf_op jit(solution)/shard_map/ppermute | solution.py:11
  12.2 2.7 fusion.18
  14.9 1.9 collective-permute-start
  16.8 6.7 %collective-permute-start.3 = (bf16[2,16,128,128]{3,2,1,0:T(8,128)(2,1)}, bf16[2,16,128,128]{3,2,1,0:T(8,128)(2,1)}, u32[]{:S(2)}, u32[]{:S(2)}) collective-permute-start(bf16[2,16,128,128]{3,2,1,0:T(8,128)(2,1)} %get-tuple-element.7), channel_id=1, source_target_pairs={{0,504},{4,508},{8,0},{12,4},{16,8},{20,12},{24,16},{28,20},{32,24... | collective-permute-start | bytes 3145736 | tf_op jit(solution)/shard_map/ppermute | solution.py:11
  26.2 144.5 %collective-permute-done = bf16[2,16,128,128]{3,2,1,0:T(8,128)(2,1)S(1)} collective-permute-done((bf16[2,16,128,128]{3,2,1,0:T(8,128)(2,1)S(1)}, bf16[2,16,128,128]{3,2,1,0:T(8,128)(2,1)S(1)}, u32[]{:S(2)}, u32[]{:S(2)}) %collective-permute-start) | collective-permute-done | bytes 1048608 | tf_op jit(solution)/shard_map/ppermute | solution.py:11
  170.7 1.1 constant_dynamic-update-slice_fusion.4
  171.8 4.1 %constant_dynamic-update-slice_fusion.3 = bf16[22,16,128,128]{3,2,1,0:T(8,128)(2,1)} fusion(bf16[22,16,128,128]{3,2,1,0:T(8,128)(2,1)} %constant_dynamic-update-slice_fusion.4, bf16[6,16,128,128]{3,2,1,0:T(8,128)(2,1)} %collective-permute-done.1), kind=kLoop, calls=%fused_computation.30 | loop fusion | bytes 6291456
  175.9 1.9 constant_dynamic-update-slice_fusion.2
  177.8 4.0 %constant_dynamic-update-slice_fusion.1 = bf16[22,16,128,128]{3,2,1,0:T(8,128)(2,1)} fusion(bf16[22,16,128,128]{3,2,1,0:T(8,128)(2,1)} %constant_dynamic-update-slice_fusion.2, bf16[6,16,128,128]{3,2,1,0:T(8,128)(2,1)} %collective-permute-done.2), kind=kLoop, calls=%fused_computation.28 | loop fusion | bytes 6291456
  181.8 51.7 %collective-permute-done.3 = bf16[2,16,128,128]{3,2,1,0:T(8,128)(2,1)} collective-permute-done((bf16[2,16,128,128]{3,2,1,0:T(8,128)(2,1)}, bf16[2,16,128,128]{3,2,1,0:T(8,128)(2,1)}, u32[]{:S(2)}, u32[]{:S(2)}) %collective-permute-start.3) | collective-permute-done | bytes 1048608 | tf_op jit(solution)/shard_map/ppermute | solution.py:11
  233.4 2.3 constant_dynamic-update-slice_fusion
  235.7 15.5 %gather_fusion.1 = bf16[384,128,128]{2,1,0:T(8,128)(2,1)} fusion(bf16[352,128,128]{2,1,0:T(8,128)(2,1)} %bitcast.1, s32[1024]{0:T(1024)S(1)} %pad_clamp_fusion), kind=kCustom, calls=%fused_computation.1 | custom fusion | bytes 25167360 | tf_op jit(solution)/shard_map/jit(_take)/gather | solution.py:30
  251.3 7.9 %fusion = f32[6,4,128,128,1]{3,2,1,4,0:T(8,128)S(1)} fusion(bf16[6,16,4,128,128]{4,3,2,1,0:T(8,128)(2,1)} %bitcast.62, pred[6,16,4]{2,1,0:T(8,128)(4,1)S(1)} %copy.51, bf16[6,16,128,128]{3,2,1,0:T(8,128)(2,1)S(1)} %copy-done), kind=kOutput, calls=%fused_computation.3 | convolution fusion | flops 1616904192 | bytes 17301888 | tf_op jit(solution)/shard_map/aixy,aijyz->ajxz/dot_general | solution.py:56
  259.3 3.1 collective-permute-start.4
  262.4 3.4 %collective-permute-start.5 = (bf16[6,4,128,128]{2,3,1,0:T(8,128)(2,1)S(1)}, bf16[6,4,128,128]{2,3,1,0:T(8,128)(2,1)S(1)}, u32[]{:S(2)}, u32[]{:S(2)}) collective-permute-start(bf16[6,4,128,128]{2,3,1,0:T(8,128)(2,1)S(1)} %fusion.13), channel_id=1, source_target_pairs={{0,3},{1,0},{2,1},{3,2},{4,7},{5,4},{6,5},{7,6},{8,11},{9,8},{10,9... | collective-permute-start | bytes 2359304 | tf_op jit(solution)/shard_map/ppermute | solution.py:70
  265.8 15.3 %collective-permute-done.4 = bf16[6,4,128,128]{2,3,1,0:T(8,128)(2,1)} collective-permute-done((bf16[6,4,128,128]{2,3,1,0:T(8,128)(2,1)S(1)}, bf16[6,4,128,128]{2,3,1,0:T(8,128)(2,1)}, u32[]{:S(2)}, u32[]{:S(2)}) %collective-permute-start.4) | collective-permute-done | bytes 786464 | tf_op jit(solution)/shard_map/ppermute | solution.py:65
  281.1 2.1 collective-permute-start.6
  283.7 2.4 broadcast_in_dim.52
  287.1 1.5 copy.55
  291.1 11.1 %collective-permute-done.6 = bf16[6,4,128,128]{2,3,1,0:T(8,128)(2,1)} collective-permute-done((bf16[6,4,128,128]{2,3,1,0:T(8,128)(2,1)}, bf16[6,4,128,128]{2,3,1,0:T(8,128)(2,1)}, u32[]{:S(2)}, u32[]{:S(2)}) %collective-permute-start.6) | collective-permute-done | bytes 786464 | tf_op jit(solution)/shard_map/ppermute | solution.py:65
  302.2 1.5 copy.57
  304.8 8.5 %fusion.10 = bf16[6,4,128,128]{2,3,1,0:T(8,128)(2,1)S(1)} fusion(bf16[6,16,128,128]{3,2,1,0:T(8,128)(2,1)} %constant_dynamic-update-slice_fusion.8, bf16[6,16,4,128,128]{4,3,2,1,0:T(8,128)(2,1)} %bitcast.63, pred[6,16,4]{2,1,0:T(8,128)(4,1)S(1)} %copy.51, f32[6,4,128,128,1]{3,2,1,4,0:T(8,128)S(1)} %copy-done.2), kind=kOutput, calls=%fused_computation.14 | convolution fusion | flops 1618477056 | bytes 18088320 | tf_op jit(solution)/shard_map/aixy,aijyz->ajxz/dot_general | solution.py:76
  313.3 1.2 copy.59
  (35 shorter events, 7.8 us)
Async XLA Ops:
  0.0 23.5 %copy-start.3 = (s32[768,16]{0,1:T(8,128)S(1)}, s32[768,16]{0,1:T(8,128)}, u32[]{:S(2)}) copy-start(s32[768,16]{0,1:T(8,128)} %param.3) | copy-start | bytes 147460
  0.0 171.8 %collective-permute-start.1 = (bf16[6,16,128,128]{3,2,1,0:T(8,128)(2,1)}, bf16[6,16,128,128]{3,2,1,0:T(8,128)(2,1)}, u32[]{:S(2)}, u32[]{:S(2)}) collective-permute-start(bf16[6,16,128,128]{3,2,1,0:T(8,128)(2,1)} %param.2), channel_id=1, source_target_pairs={{0,4},{4,8},{8,12},{12,16},{16,20},{20,24},{24,28},{28,32},{32,36}... | collective-permute-start | bytes 9437192 | tf_op jit(solution)/shard_map/ppermute | solution.py:11
  4.5 173.3 %collective-permute-start.2 = (bf16[6,16,128,128]{3,2,1,0:T(8,128)(2,1)}, bf16[6,16,128,128]{3,2,1,0:T(8,128)(2,1)}, u32[]{:S(2)}, u32[]{:S(2)}) collective-permute-start(bf16[6,16,128,128]{3,2,1,0:T(8,128)(2,1)} %param.2), channel_id=1, source_target_pairs={{0,508},{4,0},{8,4},{12,8},{16,12},{20,16},{24,20},{28,24},{32,28}... | collective-permute-start | bytes 9437192 | tf_op jit(solution)/shard_map/ppermute | solution.py:11
  14.9 155.8 %collective-permute-start = (bf16[2,16,128,128]{3,2,1,0:T(8,128)(2,1)S(1)}, bf16[2,16,128,128]{3,2,1,0:T(8,128)(2,1)S(1)}, u32[]{:S(2)}, u32[]{:S(2)}) collective-permute-start(bf16[2,16,128,128]{3,2,1,0:T(8,128)(2,1)S(1)} %get-tuple-element.8), channel_id=1, source_target_pairs={{0,8},{4,12},{8,16},{12,20},{16,24},{20,28},{24,32},{28,36},{32,40... | collective-permute-start | bytes 3145736 | tf_op jit(solution)/shard_map/ppermute | solution.py:11
  16.8 216.6 %collective-permute-start.3 = (bf16[2,16,128,128]{3,2,1,0:T(8,128)(2,1)}, bf16[2,16,128,128]{3,2,1,0:T(8,128)(2,1)}, u32[]{:S(2)}, u32[]{:S(2)}) collective-permute-start(bf16[2,16,128,128]{3,2,1,0:T(8,128)(2,1)} %get-tuple-element.7), channel_id=1, source_target_pairs={{0,504},{4,508},{8,0},{12,4},{16,8},{20,12},{24,16},{28,20},{32,24... | collective-permute-start | bytes 3145736 | tf_op jit(solution)/shard_map/ppermute | solution.py:11
  171.8 4.1 %copy-start = (bf16[6,16,128,128]{3,2,1,0:T(8,128)(2,1)S(1)}, bf16[6,16,128,128]{3,2,1,0:T(8,128)(2,1)}, u32[]{:S(2)}) copy-start(bf16[6,16,128,128]{3,2,1,0:T(8,128)(2,1)} %param.2) | copy-start | bytes 9437188
  259.1 22.0 %copy-start.1 = (f32[6,4,128,128,1]{3,2,1,4,0:T(8,128)}, f32[6,4,128,128,1]{3,2,1,4,0:T(8,128)S(1)}, u32[]{:S(2)}) copy-start(f32[6,4,128,128,1]{3,2,1,4,0:T(8,128)S(1)} %fusion) | copy-start | bytes 4718596
  259.3 21.8 %collective-permute-start.4 = (bf16[6,4,128,128]{2,3,1,0:T(8,128)(2,1)S(1)}, bf16[6,4,128,128]{2,3,1,0:T(8,128)(2,1)}, u32[]{:S(2)}, u32[]{:S(2)}) collective-permute-start(bf16[6,4,128,128]{2,3,1,0:T(8,128)(2,1)S(1)} %fusion.13), channel_id=1, source_target_pairs={{0,1},{1,2},{2,3},{3,0},{4,5},{5,6},{6,7},{7,4},{8,9},{9,10},{10,1... | collective-permute-start | bytes 2359304 | tf_op jit(solution)/shard_map/ppermute | solution.py:65
  262.4 26.3 %collective-permute-start.5 = (bf16[6,4,128,128]{2,3,1,0:T(8,128)(2,1)S(1)}, bf16[6,4,128,128]{2,3,1,0:T(8,128)(2,1)S(1)}, u32[]{:S(2)}, u32[]{:S(2)}) collective-permute-start(bf16[6,4,128,128]{2,3,1,0:T(8,128)(2,1)S(1)} %fusion.13), channel_id=1, source_target_pairs={{0,3},{1,0},{2,1},{3,2},{4,7},{5,4},{6,5},{7,6},{8,11},{9,8},{10,9... | collective-permute-start | bytes 2359304 | tf_op jit(solution)/shard_map/ppermute | solution.py:70
  281.1 21.1 %collective-permute-start.6 = (bf16[6,4,128,128]{2,3,1,0:T(8,128)(2,1)}, bf16[6,4,128,128]{2,3,1,0:T(8,128)(2,1)}, u32[]{:S(2)}, u32[]{:S(2)}) collective-permute-start(bf16[6,4,128,128]{2,3,1,0:T(8,128)(2,1)} %collective-permute-done.4), channel_id=1, source_target_pairs={{0,1},{1,2},{2,3},{3,0},{4,5},{5,6},{6,7},{7,4},{8,9},{9,10},{10,1... | collective-permute-start | bytes 2359304 | tf_op jit(solution)/shard_map/ppermute | solution.py:65
  289.1 15.8 %copy-start.2 = (f32[6,4,128,128,1]{3,2,1,4,0:T(8,128)S(1)}, f32[6,4,128,128,1]{3,2,1,4,0:T(8,128)}, u32[]{:S(2)}) copy-start(f32[6,4,128,128,1]{3,2,1,4,0:T(8,128)} %copy-done.1) | copy-start | bytes 4718596
